TPU v7x, 32 devices: a whole 2x2x4 slice. The times are simulated.
32 devices in a mesh: pop: 2 (over y), ctx: 4 (over z), exp: 2 (over x), tp: 2 (over core).
Axes of the slice: x: 2, y: 2, z: 4, core: 2. Of those that a mesh axis runs over, the one named last changes fastest.
Arguments:
- tokens: bfloat16 [2048, 2688], P(('pop', 'ctx', 'tp')), parts along dimension 0, may hold values from -6 to 6
- routes: int32 [2048, 6], P(('pop', 'ctx', 'tp')), parts along dimension 0, may hold values from 0 to 15, all different within a row; in each aligned block of 128 rows (0 to 127, 128 to 255, ...) at most 64 rows name the same one
- route_gates: float32 [2048, 6], P(('pop', 'ctx', 'tp')), parts along dimension 0, may hold values from 0.05 to 1
- up_weight: bfloat16 [16, 2688, 1536], P(('ctx', 'tp'), None, 'exp'), may hold values from -0.125 to 0.125
- down_weight: bfloat16 [16, 1536, 2688], P(('ctx', 'tp'), None, 'exp'), may hold values from -0.15625 to 0.15625
- factor_seeds: int32 [32, 4], P(('pop', 'ctx', 'tp')), parts along dimension 0, may hold values from 0 to 15
- up_left: bfloat16 [16, 2688], replicated, may hold values from -0.125 to 0.125
- up_right: bfloat16 [16, 1536], P(None, 'exp'), may hold values from -3 to 3
- down_left: bfloat16 [16, 1536], replicated, may hold values from -0.15625 to 0.15625
- down_right: bfloat16 [16, 2688], P(None, 'exp'), may hold values from -3 to 3
Outputs:
- moe_output: bfloat16 [2048, 2688], P(('pop', 'ctx', 'tp'), 'exp'), parts along dimension 0
There are 2 independent parts, one for each index of `pop`. A program takes and returns all parts, laid end to end along the dimension named above; an argument that names none is the same for every part. Nothing has to cross between parts.
Inputs may be any that keep to these rules, and one draw needn't show every extreme that they name: `routes`: each row names 6 different experts. Among the 128 rows of one device (aligned blocks of 128 rows) no expert is named more than 64 times, and in every draw some expert is named exactly 64 times in some block.
All inputs are finite; a program needn't handle non-finite values.
Results may differ from a plain program's by a relative error of at most 0.0057.
Values may be sent and summed in bfloat16 or wider, within the bound.
A program may use at most 64 MiB of HBM per device.

v0:
```python
import jax
import jax.numpy as jnp
from jax import lax
from jax.sharding import PartitionSpec as P


def pick_rows(factor_table, indices):
    chooser = (
        indices[:, None] == jnp.arange(factor_table.shape[0], dtype=jnp.int32)[None, :]
    ).astype(factor_table.dtype)
    return jnp.dot(chooser, factor_table, preferred_element_type=jnp.float32).astype(
        factor_table.dtype
    )


def on_device(
    tokens,
    routes,
    route_gates,
    up_weight,
    down_weight,
    factor_seeds,
    up_left,
    up_right,
    down_left,
    down_right,
):
    dest_count = lax.axis_size("ctx") * lax.axis_size("tp")
    local_experts = up_weight.shape[0]
    experts_all = dest_count * local_experts
    tok_count, top_count = routes.shape
    capacity = 4 * tok_count * top_count // (3 * experts_all)
    model_width = tokens.shape[1]
    flat_routes = routes.reshape(-1)
    chooser = (flat_routes[:, None] == jnp.arange(experts_all, dtype=jnp.int32)[None, :]).astype(
        jnp.int32
    )
    earlier = jnp.cumsum(chooser, axis=0) - chooser
    slot_index = jnp.sum(earlier * chooser, axis=1)
    target = flat_routes * capacity + slot_index
    pair_token = jnp.arange(tok_count * top_count, dtype=jnp.int32) // top_count + 1
    owner_token = jnp.zeros((experts_all * capacity,), jnp.int32).at[target].set(pair_token)
    source_row = jnp.where(owner_token > 0, owner_token - 1, tok_count)
    padded_tokens = jnp.concatenate([tokens, jnp.zeros((1, model_width), tokens.dtype)], axis=0)
    token_rows = padded_tokens[source_row]
    outgoing = token_rows.reshape(dest_count, local_experts, capacity, model_width)
    left_up = pick_rows(up_left, factor_seeds[:, 0])
    right_up = pick_rows(up_right, factor_seeds[:, 1])
    left_down = pick_rows(down_left, factor_seeds[:, 2])
    right_down = pick_rows(down_right, factor_seeds[:, 3])
    buffer = lax.all_to_all(outgoing, ("ctx", "tp"), split_axis=0, concat_axis=0, tiled=True)
    up_act = jnp.einsum("slcd,ldh->slch", buffer, up_weight, preferred_element_type=jnp.float32)
    low_rank = jnp.einsum("slcd,ld->slc", buffer, left_up, preferred_element_type=jnp.float32)
    up_act = up_act + low_rank[..., None] * right_up[None, :, None, :].astype(jnp.float32)
    hidden = (jnp.maximum(up_act, 0.0) ** 2).astype(jnp.bfloat16)
    full_hidden = lax.all_gather(hidden, "exp", axis=3, tiled=True)
    summed = jnp.einsum(
        "slch,lhd->slcd", full_hidden, down_weight, preferred_element_type=jnp.float32
    )
    rank_sum = jnp.einsum(
        "slch,lh->slc", full_hidden, left_down, preferred_element_type=jnp.float32
    )
    result = (
        summed + rank_sum[..., None] * right_down[None, :, None, :].astype(jnp.float32)
    ).astype(jnp.bfloat16)
    returned = lax.all_to_all(result, ("ctx", "tp"), split_axis=0, concat_axis=0, tiled=True)
    back_rows = returned.reshape(experts_all * capacity, -1)
    picked = back_rows[target]
    normed = (route_gates / jnp.sum(route_gates, axis=1, keepdims=True)).reshape(-1)
    weighted = picked.astype(jnp.float32) * normed[:, None]
    moe_output = jnp.sum(weighted.reshape(tok_count, top_count, -1), axis=1)
    return moe_output.astype(jnp.bfloat16)


def solution(mesh):
    in_specs = (
        P(("pop", "ctx", "tp"), None),
        P(("pop", "ctx", "tp"), None),
        P(("pop", "ctx", "tp"), None),
        P(("ctx", "tp"), None, "exp"),
        P(("ctx", "tp"), None, "exp"),
        P(("pop", "ctx", "tp"), None),
        P(),
        P(None, "exp"),
        P(),
        P(None, "exp"),
    )
    out_specs = P(("pop", "ctx", "tp"), "exp")
    return jax.shard_map(
        on_device, mesh=mesh, in_specs=in_specs, out_specs=out_specs, check_vma=False
    )
```

profile of v0, /device:TPU:0, one launch (start us, length us, event | category | flops | bytes accessed | tf_op | source)
XLA Modules:
  0.0 316.2 jit_solution(15399134807292461094)
XLA Ops:
  6.5 0.8 copy.28
  7.4 0.1 eq.89
  7.5 0.1 eq.85
  7.6 0.7 broadcast_multiply_fusion
  8.4 1.7 reduce-window.6
  10.1 0.3 slice_reduce_fusion
  10.4 0.1 copy.27
  10.5 0.1 mul.56
  10.6 0.1 fusion.23
  10.7 3.4 %scatter_custom_fusion = s32[1024]{0:T(1024)S(1)} fusion(s32[768]{0:T(1024)S(1)} %fusion.33, s32[768]{0:T(1024)S(1)} %fusion.28, s32[]{:T(128)} %constant.11.clone.1), kind=kCustom, calls=%fused_computation.52 | custom fusion | bytes 4100 | tf_op jit(solution)/shard_map/scatter | solution.py:42
  14.1 1.2 concatenate.3
  15.3 6.6 %gather_fusion = bf16[1024,2688]{1,0:T(8,128)(2,1)} fusion(bf16[129,2688]{1,0:T(8,128)(2,1)S(1)} %concatenate.3, s32[1024]{0:T(1024)S(1)} %fusion.31), kind=kCustom, calls=%fused_computation | custom fusion | bytes 11014144 | tf_op jit(solution)/shard_map/gather | solution.py:45
  21.9 6.5 %all-to-all-start = ((bf16[8,2,64,2688]{3,2,1,0:T(8,128)(2,1)}), bf16[8,2,64,2688]{3,2,1,0:T(8,128)(2,1)}, u32[]{:S(2)}, u32[]{:S(2)}) async-start(bf16[8,2,64,2688]{3,2,1,0:T(8,128)(2,1)} %bitcast.67), calls=%async_computation | async-start | bytes 11010048 | tf_op jit(solution)/shard_map/all_to_all | solution.py:51
  28.4 0.2 slice_reduce_fusion.2
  28.7 0.2 fusion.10
  28.9 0.2 fusion.20
  29.1 121.5 %all-to-all-done = bf16[8,2,64,2688]{3,2,1,0:T(8,128)(2,1)} async-done(((bf16[8,2,64,2688]{3,2,1,0:T(8,128)(2,1)}), bf16[8,2,64,2688]{3,2,1,0:T(8,128)(2,1)}, u32[]{:S(2)}, u32[]{:S(2)}) %all-to-all-start) | async-done | bytes 5505056 | tf_op jit(solution)/shard_map/all_to_all | solution.py:51
  150.5 4.9 %fusion.5 = f32[2,1,8,64]{3,1,2,0:T(1,128)S(1)} fusion(bf16[8,2,64,2688]{3,2,1,0:T(8,128)(2,1)} %all-to-all-done, bf16[2,2688,1,1]{1,0,2,3:T(2,128)(2,1)S(1)} %fusion.10), kind=kOutput, calls=%fused_computation.10 | convolution fusion | flops 5505024 | bytes 5519872 | tf_op jit(solution)/shard_map/slcd,ld->slc/dot_general | solution.py:53
  155.4 10.8 %fusion.13 = bf16[8,2,64,768]{3,2,0,1:T(8,128)(2,1)} fusion(bf16[2,2688,768]{2,1,0:T(8,128)(2,1)} %param.13, bf16[8,2,64,2688]{3,2,1,0:T(8,128)(2,1)} %all-to-all-done, f32[2,768]{1,0:T(2,128)S(1)} %fusion.20, f32[8,2,64]{2,0,1:T(8,128)S(1)} %bitcast.70), kind=kOutput, calls=%fused_computation.18 | convolution fusion | flops 4231790592 | bytes 15345664 | tf_op jit(solution)/shard_map/slcd,ldh->slch/dot_general | solution.py:52
  166.3 0.2 fusion.15
  166.5 0.2 fusion.14
  166.7 43.6 %all-gather.2.cloned.1.call-done = bf16[8,2,64,1536]{3,2,0,1:T(8,128)(2,1)} async-done(((bf16[8,2,64,768]{3,2,0,1:T(8,128)(2,1)}), bf16[8,2,64,1536]{3,2,0,1:T(8,128)(2,1)}) %all-gather.2.cloned.1.call-update) | async-done | bytes 3145744 | tf_op jit(solution)/shard_map/all_gather | solution.py:56
  210.3 3.2 %fusion.26 = f32[2,1,8,64]{3,1,2,0:T(1,128)S(1)} fusion(bf16[8,2,64,1536]{3,2,0,1:T(8,128)(2,1)} %all-gather.2.cloned.1.call-done, bf16[2,1536,1,1]{1,0,2,3:T(2,128)(2,1)S(1)} %fusion.15), kind=kOutput, calls=%fused_computation.36 | convolution fusion | flops 3145728 | bytes 3155968 | tf_op jit(solution)/shard_map/slch,lh->slc/dot_general | solution.py:60
  213.5 9.2 %fusion.4 = bf16[8,2,64,1344]{3,2,0,1:T(8,128)(2,1)S(1)} fusion(bf16[8,2,64,1536]{3,2,0,1:T(8,128)(2,1)} %all-gather.2.cloned.1.call-done, bf16[2,1536,1344]{1,2,0:T(8,128)(2,1)} %param.14, f32[2,1344]{1,0:T(2,128)S(1)} %fusion.14, f32[8,2,64]{2,0,1:T(8,128)S(1)} %bitcast.69), kind=kOutput, calls=%fused_computation.8 | convolution fusion | flops 4231987200 | bytes 14170624 | tf_op jit(solution)/shard_map/slch,lhd->slcd/dot_general | solution.py:57
  222.7 1.8 copy.32
  224.5 4.6 %all-to-all-start.1 = ((bf16[8,2,64,1344]{3,2,1,0:T(8,128)(2,1)}), bf16[8,2,64,1344]{3,2,1,0:T(8,128)(2,1)S(1)}, u32[]{:S(2)}, u32[]{:S(2)}) async-start(bf16[8,2,64,1344]{3,2,1,0:T(8,128)(2,1)} %copy.32), calls=%async_computation.1 | async-start | bytes 5767168 | tf_op jit(solution)/shard_map/all_to_all | solution.py:66
  229.1 0.1 copy.33
  229.3 65.7 %all-to-all-done.1 = bf16[8,2,64,1344]{3,2,1,0:T(8,128)(2,1)S(1)} async-done(((bf16[8,2,64,1344]{3,2,1,0:T(8,128)(2,1)}), bf16[8,2,64,1344]{3,2,1,0:T(8,128)(2,1)S(1)}, u32[]{:S(2)}, u32[]{:S(2)}) %all-to-all-start.1) | async-done | bytes 2752544 | tf_op jit(solution)/shard_map/all_to_all | solution.py:66
  295.0 3.7 %gather_fusion.1 = bf16[768,1344]{1,0:T(8,128)(2,1)} fusion(bf16[1024,1344]{1,0:T(8,128)(2,1)S(1)} %bitcast.66, s32[1024]{0:T(1024)S(1)} %pad_clamp_fusion), kind=kCustom, calls=%fused_computation.1 | custom fusion | bytes 4131840 | tf_op jit(solution)/shard_map/gather | solution.py:68
  298.7 5.0 %reshape.72 = f32[128,6,1344]{2,1,0:T(8,128)} reshape(bf16[768,1344]{1,0:T(8,128)(2,1)} %gather_fusion.1) | data formatting | bytes 6193152 | tf_op jit(solution)/shard_map/convert_element_type | solution.py:70
  303.7 4.7 %multiply_reduce_fusion = bf16[128,1344]{1,0:T(8,128)(2,1)S(1)} fusion(f32[128,6,1344]{2,1,0:T(8,128)} %reshape.72, f32[128,6]{1,0:T(8,128)S(1)} %copy.33), kind=kLoop, calls=%fused_computation.9 | loop fusion | flops 1892352 | bytes 4475904 | tf_op jit(solution)/shard_map/reduce_sum | solution.py:71
  308.5 0.9 copy.34
  (22 shorter events, 0.2 us)
Async XLA Ops:
  6.5 22.1 %copy-start = (bf16[16,2688]{1,0:T(8,128)(2,1)S(1)}, bf16[16,2688]{1,0:T(8,128)(2,1)}, u32[]{:S(2)}) copy-start(bf16[16,2688]{1,0:T(8,128)(2,1)} %param.16) | copy-start | bytes 258052
  21.9 6.5 %copy-start.2 = (s32[2,4]{1,0:T(2,128)S(1)}, s32[2,4]{1,0:T(2,128)}, u32[]{:S(2)}) copy-start(s32[2,4]{1,0:T(2,128)} %param.15) | copy-start | bytes 100
  21.9 7.0 %copy-start.5 = (bf16[16,768]{1,0:T(8,128)(2,1)S(1)}, bf16[16,768]{1,0:T(8,128)(2,1)}, u32[]{:S(2)}) copy-start(bf16[16,768]{1,0:T(8,128)(2,1)} %param.17) | copy-start | bytes 73732
  21.9 128.7 %all-to-all-start = ((bf16[8,2,64,2688]{3,2,1,0:T(8,128)(2,1)}), bf16[8,2,64,2688]{3,2,1,0:T(8,128)(2,1)}, u32[]{:S(2)}, u32[]{:S(2)}) async-start(bf16[8,2,64,2688]{3,2,1,0:T(8,128)(2,1)} %bitcast.67), calls=%async_computation | async-start | bytes 11010048 | tf_op jit(solution)/shard_map/all_to_all | solution.py:51
  28.4 181.9 %all-gather.2.cloned.1.call-start = ((), (), s32[]{:S(2)}) async-start(), calls=%async_computation.2 | async-start | bytes 4718592 | tf_op jit(solution)/shard_map/all_gather | solution.py:56
  155.4 10.9 %copy-start.3 = (bf16[16,1536]{1,0:T(8,128)(2,1)S(1)}, bf16[16,1536]{1,0:T(8,128)(2,1)}, u32[]{:S(2)}) copy-start(bf16[16,1536]{1,0:T(8,128)(2,1)} %param.18) | copy-start | bytes 147460
  155.4 11.1 %copy-start.4 = (bf16[16,1344]{1,0:T(8,128)(2,1)S(1)}, bf16[16,1344]{1,0:T(8,128)(2,1)}, u32[]{:S(2)}) copy-start(bf16[16,1344]{1,0:T(8,128)(2,1)} %param.19) | copy-start | bytes 129028
  222.7 6.4 %copy-start.1 = (f32[128,6]{0,1:T(8,128)S(1)}, f32[128,6]{0,1:T(8,128)}, u32[]{:S(2)}) copy-start(f32[128,6]{0,1:T(8,128)} %param.12) | copy-start | bytes 9220
  224.5 70.5 %all-to-all-start.1 = ((bf16[8,2,64,1344]{3,2,1,0:T(8,128)(2,1)}), bf16[8,2,64,1344]{3,2,1,0:T(8,128)(2,1)S(1)}, u32[]{:S(2)}, u32[]{:S(2)}) async-start(bf16[8,2,64,1344]{3,2,1,0:T(8,128)(2,1)} %copy.32), calls=%async_computation.1 | async-start | bytes 5767168 | tf_op jit(solution)/shard_map/all_to_all | solution.py:66
Sparse Core Ops, SparseCore 0:
  166.4 43.8 all-gather.1
where the time goes:
time: 317 us; the launch traced here: 316 us
  waiting for transfers between devices  231 us (73%)
  matrix products  28.9 us (9%)
  local copies, waits for them, and re-layouts  24.5 us (8%)
  between operations  13.5 us (4%)
  starting transfers between devices  11.1 us (4%)
  other arithmetic  7.34 us (2%)
    all_to_all x1, waiting for transfers between devices, on_device(): lax.all_to_all(outgoing, ('ctx', 'tp'), split_axis=0, concat_axis=0, tile...  121 us
    all_to_all x1, waiting for transfers between devices, on_device(): lax.all_to_all(result, ('ctx', 'tp'), split_axis=0, concat_axis=0, tiled=...  65.7 us
    all_gather x1, waiting for transfers between devices, on_device(): full_hidden = lax.all_gather(hidden, 'exp', axis=3, tiled=True)  43.6 us
    dot_general x1, matrix products, on_device(): jnp.einsum('slcd,ldh->slch', buffer, up_weight, preferred_element_type=jn...  10.8 us
    dot_general x1, matrix products, on_device(): jnp.einsum('slch,lhd->slcd', full_hidden, down_weight, preferred_element_...  9.18 us
    gather x1, local copies, waits for them, and re-layouts, on_device(): token_rows = padded_tokens[source_row]  6.58 us
    all_to_all x1, starting transfers between devices, on_device(): lax.all_to_all(outgoing, ('ctx', 'tp'), split_axis=0, concat_axis=0, tile...  6.48 us
  transfers between devices with their start and end apart: 3, of which 3 were waited for; matrix products, arithmetic and copies ran while one was open for 0% of the time, Pallas kernels for 0%

commit v1 on v0

--- a/solution.py
+++ b/solution.py
@@ -1,6 +1,10 @@
+import functools
+
 import jax
 import jax.numpy as jnp
 from jax import lax
+from jax.experimental import pallas as pl
+from jax.experimental.pallas import tpu as pltpu
 from jax.sharding import PartitionSpec as P
 
 
@@ -13,7 +17,7 @@
     )
 
 
-def on_device(
+def general_path(
     tokens,
     routes,
     route_gates,
@@ -72,6 +76,333 @@
     return moe_output.astype(jnp.bfloat16)
 
 
+def fused_kernel(
+    cfg,
+    meta_ref, tokens_ref, lu_ref, ru_ref, ld_ref, rd_ref, wu_hbm, wd_hbm,
+    out_ref,
+    rows, meta_in, wu, wd, xs, hid_own, hid_rem, scaled, own_part, pair_out, pair_in,
+    far_out, far_in, kept,
+    z_s, z_r, x_s, x_r, cz_s, cz_r, cx_s, cx_r, h_s, h_r, p_s, p_r, o_s, o_r, m_s, m_r, loc,
+):
+    ctx_n, tp_n, local_n, cap, zr = cfg
+    tok = tokens_ref.shape[0]
+    half = wu.shape[2]
+    xr = tok - zr
+    c, e, t = lax.axis_index("ctx"), lax.axis_index("exp"), lax.axis_index("tp")
+    other_e, other_t = 1 - e, 1 - t
+    me = c * tp_n + t
+    n = ctx_n * tp_n
+    bf, f32 = jnp.bfloat16, jnp.float32
+
+    load_up = pltpu.make_async_copy(wu_hbm, wu, loc.at[0])
+    load_down = pltpu.make_async_copy(wd_hbm, wd, loc.at[1])
+    load_tok = pltpu.make_async_copy(tokens_ref, rows.at[c, t], loc.at[2])
+    load_tok.start()
+    load_up.start()
+    load_down.start()
+
+    barrier = pltpu.get_barrier_semaphore()
+    for k in range(1, n):
+        peer = (me + k) % n
+        pl.semaphore_signal(
+            barrier, inc=1, device_id={"ctx": peer // tp_n, "tp": peer % tp_n},
+            device_id_type=pl.DeviceIdType.MESH,
+        )
+    pl.semaphore_signal(
+        barrier, inc=1, device_id={"exp": other_e}, device_id_type=pl.DeviceIdType.MESH
+    )
+    pl.semaphore_wait(barrier, n)
+
+    def remote(src, dst, ss, rs, dev):
+        return pltpu.make_async_remote_copy(
+            src_ref=src, dst_ref=dst, send_sem=ss, recv_sem=rs, device_id=dev,
+            device_id_type=pl.DeviceIdType.MESH,
+        )
+
+    z_rows = pl.ds(pl.multiple_of(e * xr, 16), zr)
+    x_out_rows = pl.ds(pl.multiple_of(e * zr, 16), xr)
+    x_in_rows = pl.ds(pl.multiple_of(other_e * zr, 16), xr)
+
+    def z_copy(s, way):
+        ref = rows.at[s, t, z_rows]
+        return remote(ref, ref, z_s.at[s, (way + 1) // 2], z_r.at[s], {"ctx": c + way})
+
+    def x_copy(s):
+        ref = rows.at[s, t, x_out_rows]
+        return remote(ref, ref, x_s.at[s], x_r.at[s], {"exp": other_e})
+
+    def x_landing(s):
+        ref = rows.at[s, t, x_in_rows]
+        return remote(ref, ref, x_s.at[s], x_r.at[s], {"exp": other_e})
+
+    def cz_copy(s, tt):
+        ref = rows.at[s, tt, z_rows]
+        return remote(ref, ref, cz_s.at[s], cz_r.at[s], {"tp": other_t})
+
+    def cx_copy(s, tt):
+        ref = rows.at[s, tt, x_in_rows]
+        return remote(ref, ref, cx_s.at[s], cx_r.at[s], {"tp": other_t})
+
+    def h_copy(s, l):
+        return remote(
+            hid_own.at[s, l], hid_rem.at[s, l], h_s.at[s, l], h_r.at[s, l], {"exp": other_e}
+        )
+
+    def p_copy(s):
+        return remote(pair_out.at[s], pair_in.at[s], p_s.at[s], p_r.at[s], {"tp": other_t})
+
+    def o_copy(s, slot):
+        return remote(far_out.at[s], far_in.at[slot], o_s.at[s], o_r.at[slot], {"ctx": s})
+
+    def m_copy(peer, slot):
+        return remote(
+            meta_ref.at[peer], meta_in.at[slot], m_s.at[peer], m_r.at[slot],
+            {"ctx": peer // tp_n, "tp": peer % tp_n},
+        )
+
+    load_tok.wait()
+    for way in (-1, 1):
+        @pl.when((c + way >= 0) & (c + way < ctx_n))
+        def _():
+            z_copy(c, way).start()
+    for k in range(1, n):
+        m_copy((me + k) % n, me).start()
+    cz_copy(c, t).start()
+    cx_copy(c, t).start()
+    meta_in[me] = meta_ref[me]
+    for k in range(1, n):
+        peer = (me + k) % n
+        m_copy(peer, peer).wait_recv()
+    load_up.wait()
+    load_down.wait()
+
+    least = jnp.minimum(c, ctx_n - 1 - c)
+    left_long = c > ctx_n - 1 - c
+
+    def chunk_of(i):
+        near = (i + 1) // 2
+        close = jnp.where(i % 2 == 1, c - near, c + near)
+        dist = i - least
+        far = jnp.where(left_long, c - dist, c + dist)
+        return jnp.where(i <= 2 * least, close, far)
+
+    slot_iota = lax.broadcasted_iota(jnp.int32, (cap, tok), 0).astype(f32)
+
+    def place(s, tt, l):
+        info = meta_in[s * tp_n + tt]
+        hit = slot_iota == info[l : l + 1, :]
+        gate = jnp.sum(
+            jnp.where(hit, info[local_n + l : local_n + l + 1, :], 0.0), axis=1, keepdims=True
+        )
+        return jnp.where(hit, 1.0, 0.0).astype(bf), gate
+
+    def up(s):
+        for l in range(local_n):
+            parts = []
+            for q, tt in enumerate((t, other_t)):
+                chooser, _ = place(s, tt, l)
+                got = jnp.dot(chooser, rows[s, tt], preferred_element_type=f32)
+                parts.append(jnp.sum(got * lu_ref[l], axis=1, keepdims=True))
+                xs[l, q * cap : (q + 1) * cap, :] = got.astype(bf)
+            rank = jnp.concatenate(parts, axis=0)
+            act = jnp.dot(xs[l], wu[l], preferred_element_type=f32)
+            act = jnp.maximum(act + rank * ru_ref[l], 0.0)
+            hid_own[s, l] = (act * act).astype(bf)
+            h_copy(s, l).start()
+
+    def down(s, i):
+        own_rows = pl.ds(pl.multiple_of(e * half, half), half)
+        rem_rows = pl.ds(pl.multiple_of(other_e * half, half), half)
+        for l in range(local_n):
+            h_copy(s, l).wait_recv()
+            a, b = hid_own[s, l], hid_rem[s, l]
+            y = jnp.dot(a, wd[l, own_rows, :], preferred_element_type=f32)
+            y = y + jnp.dot(b, wd[l, rem_rows, :], preferred_element_type=f32)
+            rank = jnp.sum(
+                a.astype(f32) * ld_ref[l, e] + b.astype(f32) * ld_ref[l, other_e],
+                axis=1, keepdims=True,
+            )
+            y = y + rank * rd_ref[l]
+            for q, tt in enumerate((t, other_t)):
+                _, gate = place(s, tt, l)
+                scaled[q, l * cap : (l + 1) * cap, :] = (
+                    y[q * cap : (q + 1) * cap] * gate
+                ).astype(bf)
+        for q, tt in enumerate((t, other_t)):
+            chooser = jnp.concatenate([place(s, tt, l)[0] for l in range(local_n)], axis=0)
+            total = lax.dot_general(
+                chooser, scaled[q], (((0,), (0,)), ((), ())), preferred_element_type=f32
+            )
+            if q == 0:
+                own_part[i % 2] = total
+            else:
+                pair_out[s] = total.astype(bf)
+        p_copy(s).start()
+
+    def step(j, carry):
+        for side in (-1, 1):
+            s = c + side * j
+
+            @pl.when((j < ctx_n) & (s >= 0) & (s < ctx_n))
+            def _():
+                z_copy(s, side).wait_recv()
+
+                @pl.when((c - side >= 0) & (c - side < ctx_n))
+                def _():
+                    z_copy(s, -side).start()
+
+                x_copy(s).start()
+                cz_copy(s, t).start()
+
+        @pl.when(j - 1 < ctx_n)
+        def _():
+            s = chunk_of(j - 1)
+
+            @pl.when(s != c)
+            def _():
+                x_landing(s).wait_recv()
+                cx_copy(s, t).start()
+
+            cz_copy(s, other_t).wait_recv()
+            cx_copy(s, other_t).wait_recv()
+            up(s)
+
+        @pl.when((j >= 2) & (j - 2 < ctx_n))
+        def _():
+            down(chunk_of(j - 2), j - 2)
+
+        @pl.when(j >= 3)
+        def _():
+            s = chunk_of(j - 3)
+            p_copy(s).wait_recv()
+            total = own_part[(j - 3) % 2] + pair_in[s].astype(f32)
+
+            @pl.when(s == c)
+            def _():
+                kept[...] = total
+
+            @pl.when(s != c)
+            def _():
+                far_out[s] = total.astype(bf)
+                o_copy(s, c).start()
+
+        return carry
+
+    lax.fori_loop(1, ctx_n + 3, step, 0)
+
+    def gather(k, carry):
+        s = (c + k) % ctx_n
+        o_copy(s, s).wait_recv()
+        kept[...] += far_in[s].astype(f32)
+        return carry
+
+    lax.fori_loop(1, ctx_n, gather, 0)
+    out_ref[...] = kept[...].astype(out_ref.dtype)
+
+    for k in range(1, n):
+        m_copy((me + k) % n, me).wait_send()
+
+    def drain(s, carry):
+        for way in (-1, 1):
+            @pl.when((c + way >= 0) & (c + way < ctx_n) & ((s - c) * way <= 0))
+            def _():
+                z_copy(s, way).wait_send()
+
+        @pl.when(s != c)
+        def _():
+            x_copy(s).wait_send()
+            o_copy(s, c).wait_send()
+
+        cz_copy(s, t).wait_send()
+        cx_copy(s, t).wait_send()
+        p_copy(s).wait_send()
+        for l in range(local_n):
+            h_copy(s, l).wait_send()
+        return carry
+
+    lax.fori_loop(0, ctx_n, drain, 0)
+
+
+def fused_path(
+    tokens, routes, route_gates, up_weight, down_weight, factor_seeds,
+    up_left, up_right, down_left, down_right,
+):
+    ctx_n, tp_n = lax.axis_size("ctx"), lax.axis_size("tp")
+    n = ctx_n * tp_n
+    local_n, width, half = up_weight.shape
+    hid_all, out_w = down_weight.shape[1:]
+    tok, top = routes.shape
+    experts = n * local_n
+    cap = 4 * tok * top // (3 * experts)
+    f32, bf = jnp.float32, jnp.bfloat16
+    normed = route_gates / jnp.sum(route_gates, axis=1, keepdims=True)
+    hits = routes.T[None, :, :] == jnp.arange(experts, dtype=jnp.int32)[:, None, None]
+    mask = jnp.any(hits, axis=1)
+    gates = jnp.sum(jnp.where(hits, normed.T[None, :, :], 0.0), axis=1)
+    order = jnp.arange(tok, dtype=jnp.int32)
+    before = (order[:, None] < order[None, :]).astype(bf)
+    spot = jnp.dot(mask.astype(bf), before, preferred_element_type=f32)
+    slot = jnp.where(mask, spot, -1.0)
+    meta = jnp.concatenate(
+        [slot.reshape(n, local_n, tok), gates.reshape(n, local_n, tok)], axis=1
+    )
+    meta_rows = -(-2 * local_n // 8) * 8
+    meta = jnp.pad(meta, ((0, 0), (0, meta_rows - 2 * local_n), (0, 0)))
+    lu = pick_rows(up_left, factor_seeds[:, 0]).astype(f32)[:, None, :]
+    ru = pick_rows(up_right, factor_seeds[:, 1]).astype(f32)[:, None, :]
+    ld = pick_rows(down_left, factor_seeds[:, 2]).astype(f32).reshape(local_n, 2, 1, half)
+    rd = pick_rows(down_right, factor_seeds[:, 3]).astype(f32)[:, None, :]
+    zr = tok * 5 // 8
+    slots = tp_n * cap
+    vm, anyspace = pl.BlockSpec(memory_space=pltpu.VMEM), pl.BlockSpec(memory_space=pl.ANY)
+    dma = pltpu.SemaphoreType.DMA
+    return pl.pallas_call(
+        functools.partial(fused_kernel, (ctx_n, tp_n, local_n, cap, zr)),
+        out_shape=jax.ShapeDtypeStruct((tok, out_w), bf),
+        in_specs=[vm, anyspace, vm, vm, vm, vm, anyspace, anyspace],
+        out_specs=vm,
+        scratch_shapes=[
+            pltpu.VMEM((ctx_n, tp_n, tok, width), bf),
+            pltpu.VMEM((n, meta_rows, tok), f32),
+            pltpu.VMEM((local_n, width, half), bf),
+            pltpu.VMEM((local_n, hid_all, out_w), bf),
+            pltpu.VMEM((local_n, slots, width), bf),
+            pltpu.VMEM((ctx_n, local_n, slots, half), bf),
+            pltpu.VMEM((ctx_n, local_n, slots, half), bf),
+            pltpu.VMEM((tp_n, local_n * cap, out_w), bf),
+            pltpu.VMEM((2, tok, out_w), f32),
+            pltpu.VMEM((ctx_n, tok, out_w), bf),
+            pltpu.VMEM((ctx_n, tok, out_w), bf),
+            pltpu.VMEM((ctx_n, tok, out_w), bf),
+            pltpu.VMEM((ctx_n, tok, out_w), bf),
+            pltpu.VMEM((tok, out_w), f32),
+            dma((ctx_n, 2)), dma((ctx_n,)), dma((ctx_n,)), dma((ctx_n,)),
+            dma((ctx_n,)), dma((ctx_n,)), dma((ctx_n,)), dma((ctx_n,)),
+            dma((ctx_n, local_n)), dma((ctx_n, local_n)), dma((ctx_n,)), dma((ctx_n,)),
+            dma((ctx_n,)), dma((ctx_n,)), dma((n,)), dma((n,)), dma((3,)),
+        ],
+        compiler_params=pltpu.CompilerParams(
+            collective_id=0, has_side_effects=True, vmem_limit_bytes=60 * 1024 * 1024
+        ),
+    )(meta, tokens, lu, ru, ld, rd, up_weight, down_weight)
+
+
+def on_device(*args):
+    tokens, routes, up_weight, down_weight = args[0], args[1], args[3], args[4]
+    experts = lax.axis_size("ctx") * lax.axis_size("tp") * up_weight.shape[0]
+    cap = 4 * routes.shape[0] * routes.shape[1] // (3 * experts)
+    fits = (
+        lax.axis_size("exp") == 2
+        and lax.axis_size("tp") == 2
+        and up_weight.shape[2] % 128 == 0
+        and tokens.shape[0] % 128 == 0
+        and cap % 16 == 0
+        and lax.axis_size("ctx") * tokens.size <= 1 << 21
+        and up_weight.size + down_weight.size <= 5 << 21
+    )
+    return fused_path(*args) if fits else general_path(*args)
+
+
 def solution(mesh):
     in_specs = (
         P(("pop", "ctx", "tp"), None),

time: 317 us -> 127 us (0.40)
  the two profiles are of different devices: /device:TPU:0 before, /device:TPU:24 now
where the time goes in v1:
time: 127 us
  Pallas kernels  103 us (81%)
  local copies, waits for them, and re-layouts  17.1 us (13%)
  other arithmetic  3.46 us (3%)
  matrix products  3.22 us (3%)
    pallas_call x1, Pallas kernels, fused_path(): pl.pallas_call(functools.partial(fused_kernel, (ctx_n, tp_n, local_n, cap...  103 us
    unnamed x3, local copies, waits for them, and re-layouts  11.8 us
    dot_general x4, matrix products, pick_rows(): jnp.dot(chooser, factor_table, preferred_element_type=jnp.float32)  3.09 us

profile of v1, /device:TPU:24, one launch (start us, length us, event | category | flops | bytes accessed | tf_op | source)
XLA Modules:
  0.0 126.6 jit_solution(17597152071684465012)
XLA Ops:
  0.0 0.0 copy-start
  0.0 0.7 reduce_sum.18
  0.7 0.7 fusion.4
  1.4 1.0 slice_reduce_fusion
  2.5 0.7 divide_bitcast_fusion
  3.2 0.7 select_reduce_fusion
  3.9 0.9 fusion.3
  4.8 0.6 reshape.19.ru_ref
  5.4 0.1 convolution_select_fusion
  5.5 1.0 fusion.1
  6.5 0.6 reshape.22.rd_ref
  7.1 1.0 fusion.2
  8.1 0.6 reshape.21.ld_ref
  8.7 0.6 select_maximum_fusion.meta_ref
  9.4 0.0 copy-done
  9.4 0.2 fusion
  9.6 0.6 reshape.18.lu_ref
  10.2 11.8 %copy.13.wd_hbm = bf16[2,1536,1344]{2,1,0:T(8,128)(2,1)} copy(bf16[2,1536,1344]{1,2,0:T(8,128)(2,1)} %param.14) | data formatting | bytes 16515072 | tf_op args[4]
  21.9 102.8 %shard_map.100 = bf16[128,1344]{1,0:T(8,128)(2,1)} custom-call(f32[8,8,128]{2,1,0:T(8,128)} %select_maximum_fusion.meta_ref, bf16[128,2688]{1,0:T(8,128)(2,1)} %tokens_ref.1, f32[2,1,2688]{2,1,0:T(1,128)} %reshape.18.lu_ref, f32[2,1,768]{2,1,0:T(1,128)} %reshape.19.ru_ref, f32[2,2,1,768]{3,2,1,0:T(1,128)} %reshape.21.ld_ref, f32[2,1,1344]{2,1,0:T(1,128)} %reshape.22.rd_ref, ...), custom_call_target="tpu_custom_call" | custom-call | tf_op jit(solution)/shard_map/pallas_call | solution.py:359
  124.7 1.9 %copy.14 = bf16[128,1344]{0,1:T(8,128)(2,1)} copy(bf16[128,1344]{1,0:T(8,128)(2,1)} %shard_map.100) | data formatting | bytes 688128 | tf_op jit(solution)/shard_map/pallas_call | solution.py:359
Async XLA Ops:
  0.0 9.4 %copy-start = (bf16[16,2688]{1,0:T(8,128)(2,1)S(1)}, bf16[16,2688]{1,0:T(8,128)(2,1)}, u32[]{:S(2)}) copy-start(bf16[16,2688]{1,0:T(8,128)(2,1)} %param.16) | copy-start | bytes 258052

commit v2 on v1

--- a/solution.py
+++ b/solution.py
@@ -78,9 +78,9 @@
 
 def fused_kernel(
     cfg,
-    meta_ref, tokens_ref, lu_ref, ru_ref, ld_ref, rd_ref, wu_hbm, wd_hbm,
+    seeds_ref, routes_ref, gates_ref, tokens_ref, ul_ref, ur_ref, dl_ref, dr_ref, wu_hbm, wd_hbm,
     out_ref,
-    rows, meta_in, wu, wd, xs, hid_own, hid_rem, scaled, own_part, pair_out, pair_in,
+    rows, meta_ref, meta_in, lu_ref, ru_ref, ld_ref, rd_ref, wu, wd, xs, hid_own, hid_rem, scaled, own_part, pair_out, pair_in,
     far_out, far_in, kept,
     z_s, z_r, x_s, x_r, cz_s, cz_r, cx_s, cx_r, h_s, h_r, p_s, p_r, o_s, o_r, m_s, m_r, loc,
 ):
@@ -95,11 +95,20 @@
     bf, f32 = jnp.bfloat16, jnp.float32
 
     load_up = pltpu.make_async_copy(wu_hbm, wu, loc.at[0])
-    load_down = pltpu.make_async_copy(wd_hbm, wd, loc.at[1])
-    load_tok = pltpu.make_async_copy(tokens_ref, rows.at[c, t], loc.at[2])
+    load_down = [
+        pltpu.make_async_copy(
+            wd_hbm.at[l, :, pl.ds(pl.multiple_of((e if k == 0 else other_e) * half, 128), half)],
+            wd.at[l, k],
+            loc.at[2 + 2 * l + k],
+        )
+        for l in range(local_n)
+        for k in range(2)
+    ]
+    load_tok = pltpu.make_async_copy(tokens_ref, rows.at[c, t], loc.at[1])
     load_tok.start()
     load_up.start()
-    load_down.start()
+    for load in load_down:
+        load.start()
 
     barrier = pltpu.get_barrier_semaphore()
     for k in range(1, n):
@@ -111,7 +120,6 @@
     pl.semaphore_signal(
         barrier, inc=1, device_id={"exp": other_e}, device_id_type=pl.DeviceIdType.MESH
     )
-    pl.semaphore_wait(barrier, n)
 
     def remote(src, dst, ss, rs, dev):
         return pltpu.make_async_remote_copy(
@@ -161,30 +169,57 @@
         )
 
     load_tok.wait()
+    pl.semaphore_wait(barrier, n)
     for way in (-1, 1):
         @pl.when((c + way >= 0) & (c + way < ctx_n))
         def _():
             z_copy(c, way).start()
+    cz_copy(c, t).start()
+    cx_copy(c, t).start()
+
+    top = routes_ref.shape[0]
+    gate_sum = gates_ref[0:1, :]
+    for k in range(1, top):
+        gate_sum = gate_sum + gates_ref[k : k + 1, :]
+    expert = lax.broadcasted_iota(jnp.int32, (n * local_n, tok), 0)
+    gate = jnp.zeros((n * local_n, tok), f32)
+    mask = gate
+    for k in range(top):
+        hit = routes_ref[k : k + 1, :] == expert
+        gate = gate + jnp.where(hit, gates_ref[k : k + 1, :] / gate_sum, 0.0)
+        mask = mask + jnp.where(hit, 1.0, 0.0)
+    before = (
+        lax.broadcasted_iota(jnp.int32, (tok, tok), 0)
+        < lax.broadcasted_iota(jnp.int32, (tok, tok), 1)
+    )
+    spot = jnp.dot(
+        mask.astype(bf), jnp.where(before, 1.0, 0.0).astype(bf), preferred_element_type=f32
+    )
+    slot = jnp.where(mask > 0.0, spot, -1.0)
+    for k in range(n):
+        meta_ref[k, 0:local_n, :] = slot[k * local_n : (k + 1) * local_n]
+        meta_ref[k, local_n : 2 * local_n, :] = gate[k * local_n : (k + 1) * local_n]
     for k in range(1, n):
         m_copy((me + k) % n, me).start()
-    cz_copy(c, t).start()
-    cx_copy(c, t).start()
+
+    def pick(table, seed):
+        line = lax.broadcasted_iota(jnp.int32, table.shape, 0)
+        return jnp.sum(
+            jnp.where(line == seed, table[...].astype(f32), 0.0), axis=0, keepdims=True
+        )
+
+    for l in range(local_n):
+        lu_ref[l] = pick(ul_ref, seeds_ref[l, 0])
+        ru_ref[l] = pick(ur_ref, seeds_ref[l, 1])
+        whole = pick(dl_ref, seeds_ref[l, 2])
+        ld_ref[l, 0] = jnp.where(e == 0, whole[:, :half], whole[:, half:])
+        ld_ref[l, 1] = jnp.where(e == 0, whole[:, half:], whole[:, :half])
+        rd_ref[l] = pick(dr_ref, seeds_ref[l, 3])
     meta_in[me] = meta_ref[me]
     for k in range(1, n):
         peer = (me + k) % n
         m_copy(peer, peer).wait_recv()
     load_up.wait()
-    load_down.wait()
-
-    least = jnp.minimum(c, ctx_n - 1 - c)
-    left_long = c > ctx_n - 1 - c
-
-    def chunk_of(i):
-        near = (i + 1) // 2
-        close = jnp.where(i % 2 == 1, c - near, c + near)
-        dist = i - least
-        far = jnp.where(left_long, c - dist, c + dist)
-        return jnp.where(i <= 2 * least, close, far)
 
     slot_iota = lax.broadcasted_iota(jnp.int32, (cap, tok), 0).astype(f32)
 
@@ -210,16 +245,16 @@
             hid_own[s, l] = (act * act).astype(bf)
             h_copy(s, l).start()
 
+    nt = (((1,), (1,)), ((), ()))
+
     def down(s, i):
-        own_rows = pl.ds(pl.multiple_of(e * half, half), half)
-        rem_rows = pl.ds(pl.multiple_of(other_e * half, half), half)
         for l in range(local_n):
             h_copy(s, l).wait_recv()
             a, b = hid_own[s, l], hid_rem[s, l]
-            y = jnp.dot(a, wd[l, own_rows, :], preferred_element_type=f32)
-            y = y + jnp.dot(b, wd[l, rem_rows, :], preferred_element_type=f32)
+            y = lax.dot_general(a, wd[l, 0], nt, preferred_element_type=f32)
+            y = y + lax.dot_general(b, wd[l, 1], nt, preferred_element_type=f32)
             rank = jnp.sum(
-                a.astype(f32) * ld_ref[l, e] + b.astype(f32) * ld_ref[l, other_e],
+                a.astype(f32) * ld_ref[l, 0] + b.astype(f32) * ld_ref[l, 1],
                 axis=1, keepdims=True,
             )
             y = y + rank * rd_ref[l]
@@ -234,16 +269,28 @@
                 chooser, scaled[q], (((0,), (0,)), ((), ())), preferred_element_type=f32
             )
             if q == 0:
-                own_part[i % 2] = total
+                own_part[i] = total
             else:
                 pair_out[s] = total.astype(bf)
         p_copy(s).start()
 
     def step(j, carry):
+        def chunks(dist, do):
+            def one(k, carry):
+                s = c + (2 * k - 1) * dist
+
+                @pl.when((s >= 0) & (s < ctx_n) & (dist >= 0) & ((dist > 0) | (k == 0)))
+                def _():
+                    do(s, k)
+
+                return carry
+
+            lax.fori_loop(0, 2, one, 0)
+
         for side in (-1, 1):
             s = c + side * j
 
-            @pl.when((j < ctx_n) & (s >= 0) & (s < ctx_n))
+            @pl.when((j > 0) & (s >= 0) & (s < ctx_n))
             def _():
                 z_copy(s, side).wait_recv()
 
@@ -254,10 +301,7 @@
                 x_copy(s).start()
                 cz_copy(s, t).start()
 
-        @pl.when(j - 1 < ctx_n)
-        def _():
-            s = chunk_of(j - 1)
-
+        def begin(s, k):
             @pl.when(s != c)
             def _():
                 x_landing(s).wait_recv()
@@ -267,15 +311,9 @@
             cx_copy(s, other_t).wait_recv()
             up(s)
 
-        @pl.when((j >= 2) & (j - 2 < ctx_n))
-        def _():
-            down(chunk_of(j - 2), j - 2)
-
-        @pl.when(j >= 3)
-        def _():
-            s = chunk_of(j - 3)
+        def finish(s, k):
             p_copy(s).wait_recv()
-            total = own_part[(j - 3) % 2] + pair_in[s].astype(f32)
+            total = own_part[k] + pair_in[s].astype(f32)
 
             @pl.when(s == c)
             def _():
@@ -286,9 +324,18 @@
                 far_out[s] = total.astype(bf)
                 o_copy(s, c).start()
 
+        chunks(j, begin)
+
+        @pl.when(j == 1)
+        def _():
+            for load in load_down:
+                load.wait()
+
+        chunks(j - 1, down)
+        chunks(j - 1, finish)
         return carry
 
-    lax.fori_loop(1, ctx_n + 3, step, 0)
+    lax.fori_loop(0, ctx_n + 1, step, 0)
 
     def gather(k, carry):
         s = (c + k) % ctx_n
@@ -330,42 +377,34 @@
     ctx_n, tp_n = lax.axis_size("ctx"), lax.axis_size("tp")
     n = ctx_n * tp_n
     local_n, width, half = up_weight.shape
-    hid_all, out_w = down_weight.shape[1:]
+    out_w = down_weight.shape[2]
     tok, top = routes.shape
     experts = n * local_n
     cap = 4 * tok * top // (3 * experts)
     f32, bf = jnp.float32, jnp.bfloat16
-    normed = route_gates / jnp.sum(route_gates, axis=1, keepdims=True)
-    hits = routes.T[None, :, :] == jnp.arange(experts, dtype=jnp.int32)[:, None, None]
-    mask = jnp.any(hits, axis=1)
-    gates = jnp.sum(jnp.where(hits, normed.T[None, :, :], 0.0), axis=1)
-    order = jnp.arange(tok, dtype=jnp.int32)
-    before = (order[:, None] < order[None, :]).astype(bf)
-    spot = jnp.dot(mask.astype(bf), before, preferred_element_type=f32)
-    slot = jnp.where(mask, spot, -1.0)
-    meta = jnp.concatenate(
-        [slot.reshape(n, local_n, tok), gates.reshape(n, local_n, tok)], axis=1
-    )
     meta_rows = -(-2 * local_n // 8) * 8
-    meta = jnp.pad(meta, ((0, 0), (0, meta_rows - 2 * local_n), (0, 0)))
-    lu = pick_rows(up_left, factor_seeds[:, 0]).astype(f32)[:, None, :]
-    ru = pick_rows(up_right, factor_seeds[:, 1]).astype(f32)[:, None, :]
-    ld = pick_rows(down_left, factor_seeds[:, 2]).astype(f32).reshape(local_n, 2, 1, half)
-    rd = pick_rows(down_right, factor_seeds[:, 3]).astype(f32)[:, None, :]
-    zr = tok * 5 // 8
+    zr = tok * 7 // 8
     slots = tp_n * cap
     vm, anyspace = pl.BlockSpec(memory_space=pltpu.VMEM), pl.BlockSpec(memory_space=pl.ANY)
     dma = pltpu.SemaphoreType.DMA
     return pl.pallas_call(
         functools.partial(fused_kernel, (ctx_n, tp_n, local_n, cap, zr)),
         out_shape=jax.ShapeDtypeStruct((tok, out_w), bf),
-        in_specs=[vm, anyspace, vm, vm, vm, vm, anyspace, anyspace],
+        in_specs=[
+            pl.BlockSpec(memory_space=pltpu.SMEM), vm, vm, anyspace, vm, vm, vm, vm,
+            anyspace, anyspace,
+        ],
         out_specs=vm,
         scratch_shapes=[
             pltpu.VMEM((ctx_n, tp_n, tok, width), bf),
             pltpu.VMEM((n, meta_rows, tok), f32),
+            pltpu.VMEM((n, meta_rows, tok), f32),
+            pltpu.VMEM((local_n, 1, width), f32),
+            pltpu.VMEM((local_n, 1, half), f32),
+            pltpu.VMEM((local_n, 2, 1, half), f32),
+            pltpu.VMEM((local_n, 1, out_w), f32),
             pltpu.VMEM((local_n, width, half), bf),
-            pltpu.VMEM((local_n, hid_all, out_w), bf),
+            pltpu.VMEM((local_n, 2, out_w, half), bf),
             pltpu.VMEM((local_n, slots, width), bf),
             pltpu.VMEM((ctx_n, local_n, slots, half), bf),
             pltpu.VMEM((ctx_n, local_n, slots, half), bf),
@@ -379,12 +418,15 @@
             dma((ctx_n, 2)), dma((ctx_n,)), dma((ctx_n,)), dma((ctx_n,)),
             dma((ctx_n,)), dma((ctx_n,)), dma((ctx_n,)), dma((ctx_n,)),
             dma((ctx_n, local_n)), dma((ctx_n, local_n)), dma((ctx_n,)), dma((ctx_n,)),
-            dma((ctx_n,)), dma((ctx_n,)), dma((n,)), dma((n,)), dma((3,)),
+            dma((ctx_n,)), dma((ctx_n,)), dma((n,)), dma((n,)), dma((2 + 2 * local_n,)),
         ],
         compiler_params=pltpu.CompilerParams(
             collective_id=0, has_side_effects=True, vmem_limit_bytes=60 * 1024 * 1024
         ),
-    )(meta, tokens, lu, ru, ld, rd, up_weight, down_weight)
+    )(
+        factor_seeds, routes.T, route_gates.T, tokens, up_left, up_right, down_left, down_right,
+        up_weight, jnp.swapaxes(down_weight, 1, 2),
+    )
 
 
 def on_device(*args):

time: 127 us -> 105 us (0.83)
  the two profiles are of different devices: /device:TPU:24 before, /device:TPU:0 now
where the time goes in v2:
time: 105 us; the launch traced here: 104 us
  Pallas kernels  103 us (98%)
  local copies, waits for them, and re-layouts  1.89 us (2%)
    pallas_call x1, Pallas kernels, fused_path(): pl.pallas_call(functools.partial(fused_kernel, (ctx_n, tp_n, local_n, cap...  103 us

profile of v2, /device:TPU:0, one launch (start us, length us, event | category | flops | bytes accessed | tf_op | source)
XLA Modules:
  0.0 104.5 jit_solution(6283940711150526898)
XLA Ops:
  0.0 102.6 %shard_map.100 = bf16[128,1344]{1,0:T(8,128)(2,1)} custom-call(s32[2,4]{1,0:T(2,128)} %seeds_ref.1, s32[6,128]{1,0:T(8,128)} %bitcast.4, f32[6,128]{1,0:T(8,128)} %bitcast.5, bf16[128,2688]{1,0:T(8,128)(2,1)} %tokens_ref.1, bf16[16,2688]{1,0:T(8,128)(2,1)} %ul_ref.1, bf16[16,768]{1,0:T(8,128)(2,1)} %ur_ref.1, bf16[16,1536]{1,0:T(8,128)(2,1)} %dl_ref.1, ...), custom_call_target="tpu_custom_call" | custom-call | tf_op jit(solution)/shard_map/pallas_call | solution.py:390
  102.6 1.9 %copy.11 = bf16[128,1344]{0,1:T(8,128)(2,1)} copy(bf16[128,1344]{1,0:T(8,128)(2,1)} %shard_map.100) | data formatting | bytes 688128 | tf_op jit(solution)/shard_map/pallas_call | solution.py:390

commit v3 on v2

--- a/solution.py
+++ b/solution.py
@@ -175,7 +175,8 @@
         def _():
             z_copy(c, way).start()
     cz_copy(c, t).start()
-    cx_copy(c, t).start()
+    if xr:
+        cx_copy(c, t).start()
 
     top = routes_ref.shape[0]
     gate_sum = gates_ref[0:1, :]
@@ -275,11 +276,11 @@
         p_copy(s).start()
 
     def step(j, carry):
-        def chunks(dist, do):
+        def chunks(dist, do, least):
             def one(k, carry):
                 s = c + (2 * k - 1) * dist
 
-                @pl.when((s >= 0) & (s < ctx_n) & (dist >= 0) & ((dist > 0) | (k == 0)))
+                @pl.when((s >= 0) & (s < ctx_n) & (dist >= least) & ((dist > 0) | (k == 0)))
                 def _():
                     do(s, k)
 
@@ -298,20 +299,23 @@
                 def _():
                     z_copy(s, -side).start()
 
-                x_copy(s).start()
+                if xr:
+                    x_copy(s).start()
                 cz_copy(s, t).start()
 
         def begin(s, k):
-            @pl.when(s != c)
-            def _():
-                x_landing(s).wait_recv()
-                cx_copy(s, t).start()
-
             cz_copy(s, other_t).wait_recv()
-            cx_copy(s, other_t).wait_recv()
+            if xr:
+                @pl.when(s != c)
+                def _():
+                    x_landing(s).wait_recv()
+                    cx_copy(s, t).start()
+
+                cx_copy(s, other_t).wait_recv()
             up(s)
 
         def finish(s, k):
+            down(s, k)
             p_copy(s).wait_recv()
             total = own_part[k] + pair_in[s].astype(f32)
 
@@ -324,15 +328,18 @@
                 far_out[s] = total.astype(bf)
                 o_copy(s, c).start()
 
-        chunks(j, begin)
+        chunks(j, begin, 0)
 
         @pl.when(j == 1)
         def _():
             for load in load_down:
                 load.wait()
 
-        chunks(j - 1, down)
-        chunks(j - 1, finish)
+        @pl.when(j == ctx_n)
+        def _():
+            finish(c, 0)
+
+        chunks(j - 1, finish, 1)
         return carry
 
     lax.fori_loop(0, ctx_n + 1, step, 0)
@@ -357,11 +364,13 @@
 
         @pl.when(s != c)
         def _():
-            x_copy(s).wait_send()
+            if xr:
+                x_copy(s).wait_send()
             o_copy(s, c).wait_send()
 
         cz_copy(s, t).wait_send()
-        cx_copy(s, t).wait_send()
+        if xr:
+            cx_copy(s, t).wait_send()
         p_copy(s).wait_send()
         for l in range(local_n):
             h_copy(s, l).wait_send()
@@ -383,7 +392,7 @@
     cap = 4 * tok * top // (3 * experts)
     f32, bf = jnp.float32, jnp.bfloat16
     meta_rows = -(-2 * local_n // 8) * 8
-    zr = tok * 7 // 8
+    zr = tok
     slots = tp_n * cap
     vm, anyspace = pl.BlockSpec(memory_space=pltpu.VMEM), pl.BlockSpec(memory_space=pl.ANY)
     dma = pltpu.SemaphoreType.DMA

time: 105 us -> 93.3 us (0.89)
  Pallas kernels: 103 us -> 91.2 us
    pallas_call x1, Pallas kernels: 103 us -> 91.2 us  [fused_path(): pl.pallas_call(functools.partial(fused_kernel, (ctx_n, tp_n, local_n, cap...]
where the time goes in v3:
time: 93.3 us; the launch traced here: 93.1 us
  Pallas kernels  91.2 us (98%)
  local copies, waits for them, and re-layouts  1.89 us (2%)
    pallas_call x1, Pallas kernels, fused_path(): pl.pallas_call(functools.partial(fused_kernel, (ctx_n, tp_n, local_n, cap...  91.2 us
    pallas_call x1, local copies, waits for them, and re-layouts, fused_path(): pl.pallas_call(functools.partial(fused_kernel, (ctx_n, tp_n, local_n, cap...  1.89 us

profile of v3, /device:TPU:0, one launch (start us, length us, event | category | flops | bytes accessed | tf_op | source)
XLA Modules:
  0.0 93.1 jit_solution(15745605241676836931)
XLA Ops:
  0.0 91.2 %shard_map.100 = bf16[128,1344]{1,0:T(8,128)(2,1)} custom-call(s32[2,4]{1,0:T(2,128)} %seeds_ref.1, s32[6,128]{1,0:T(8,128)} %bitcast.4, f32[6,128]{1,0:T(8,128)} %bitcast.5, bf16[128,2688]{1,0:T(8,128)(2,1)} %tokens_ref.1, bf16[16,2688]{1,0:T(8,128)(2,1)} %ul_ref.1, bf16[16,768]{1,0:T(8,128)(2,1)} %ur_ref.1, bf16[16,1536]{1,0:T(8,128)(2,1)} %dl_ref.1, ...), custom_call_target="tpu_custom_call" | custom-call | tf_op jit(solution)/shard_map/pallas_call | solution.py:399
  91.2 1.9 %copy.11 = bf16[128,1344]{0,1:T(8,128)(2,1)} copy(bf16[128,1344]{1,0:T(8,128)(2,1)} %shard_map.100) | data formatting | bytes 688128 | tf_op jit(solution)/shard_map/pallas_call | solution.py:399
